TPU v7x, 32 devices: a whole 2x2x4 slice. The times are simulated.
32 devices in a mesh: dp: 8 (over z, x), tensor: 4 (over y, core).
Axes of the slice: x: 2, y: 2, z: 4, core: 2. Of those that a mesh axis runs over, the one named last changes fastest.
Arguments:
- frames: bfloat16 [12288, 768], P(('dp', 'tensor')), may hold values from -6 to 6
- segments: int32 [8, 1536], P('dp'), may hold values from 0 to 15, never falling along the last dimension, each value on 1 to 768 neighbouring positions
- norm1_gain: float32 [768], P(('dp', 'tensor')), may hold values from 0.25 to 1.75
- norm1_shift: float32 [768], P(('dp', 'tensor')), may hold values from -1.5 to 1.5
- in_weight: bfloat16 [768, 3, 768], P('dp', None, 'tensor'), may hold values from -0.21875 to 0.21875
- proj_bias: bfloat16 [2, 12, 64], P(None, 'tensor', 'dp'), may hold values from -1.5 to 1.5
- out_weight: bfloat16 [768, 768], P('tensor', 'dp'), may hold values from -0.875 to 0.875
- out_bias: float32 [768], P(('dp', 'tensor')), may hold values from -1.5 to 1.5
- norm2_gain: float32 [768], P(('dp', 'tensor')), may hold values from 0.25 to 1.75
- norm2_shift: float32 [768], P(('dp', 'tensor')), may hold values from -1.5 to 1.5
- fc1_weight: bfloat16 [768, 3072], P('dp', 'tensor'), may hold values from -0.21875 to 0.21875
- fc1_bias: bfloat16 [48, 64], P('tensor', 'dp'), may hold values from -1.5 to 1.5
- fc2_weight: bfloat16 [3072, 768], P('tensor', 'dp'), may hold values from -0.109375 to 0.109375
- fc2_bias: float32 [768], P(('dp', 'tensor')), may hold values from -1.5 to 1.5
- cotangent: bfloat16 [12288, 768], P(('dp', 'tensor')), may hold values from -6 to 6
Outputs:
- output: bfloat16 [12288, 768], P(('dp', 'tensor'))
- grad_frames: float32 [12288, 768], P(('dp', 'tensor'))
- grad_norm1_gain: float32 [768], P(('dp', 'tensor'))
- grad_norm1_shift: float32 [768], P(('dp', 'tensor'))
- grad_in_weight: float32 [768, 3, 768], P('dp', None, 'tensor')
- grad_proj_bias: float32 [2, 12, 64], P(None, 'tensor', 'dp')
- grad_out_weight: float32 [768, 768], P('tensor', 'dp')
- grad_out_bias: float32 [768], P(('dp', 'tensor'))
- grad_norm2_gain: float32 [768], P(('dp', 'tensor'))
- grad_norm2_shift: float32 [768], P(('dp', 'tensor'))
- grad_fc1_weight: float32 [768, 3072], P('dp', 'tensor')
- grad_fc1_bias: float32 [48, 64], P('tensor', 'dp')
- grad_fc2_weight: float32 [3072, 768], P('tensor', 'dp')
- grad_fc2_bias: float32 [768], P(('dp', 'tensor'))
Inputs may be any that keep to these rules, and one draw needn't show every extreme that they name: `segments`: within each sequence the numbers never fall, every number appears, each covers 1 to 768 frames, and one covers exactly 768.
All inputs are finite; a program needn't handle non-finite values.
Results may differ from a plain program's by a relative error of at most 0.015.
Values may be sent and summed in bfloat16 or wider, within the bound.
A program may use at most 128 MiB of HBM per device.

v0:
```python
import jax
import jax.numpy as jnp
from jax import lax
from jax.sharding import PartitionSpec as P

HD = 64


def layer_norm(row_block, norm_gain, norm_shift):
    row_mean = jnp.mean(row_block, axis=-1, keepdims=True)
    centred = row_block - row_mean
    row_var = jnp.mean(centred * centred, axis=-1, keepdims=True)
    return centred * lax.rsqrt(row_var + 1e-05) * norm_gain + norm_shift


def gelu_exact(values_in):
    return jax.nn.gelu(values_in, approximate=False)


def contract(pattern, left, right):
    return jnp.einsum(pattern, left, right, preferred_element_type=jnp.float32)


def on_device(
    frames,
    segments,
    norm1_gain,
    norm1_shift,
    in_weight,
    proj_bias,
    out_weight,
    out_bias,
    norm2_gain,
    norm2_shift,
    fc1_weight,
    fc1_bias,
    fc2_weight,
    fc2_bias,
    cotangent,
):
    gain_one, shift_one, gain_two, shift_two, bias_out, bias_fc2 = (
        lax.all_gather(norm1_gain, ("dp", "tensor"), axis=0, tiled=True),
        lax.all_gather(norm1_shift, ("dp", "tensor"), axis=0, tiled=True),
        lax.all_gather(norm2_gain, ("dp", "tensor"), axis=0, tiled=True),
        lax.all_gather(norm2_shift, ("dp", "tensor"), axis=0, tiled=True),
        lax.all_gather(out_bias, ("dp", "tensor"), axis=0, tiled=True),
        lax.all_gather(fc2_bias, ("dp", "tensor"), axis=0, tiled=True),
    )
    in_full, proj_full, out_full, fc1_full, fc1b_full, fc2_full = (
        lax.all_gather(in_weight, "dp", axis=0, tiled=True),
        lax.all_gather(proj_bias, "dp", axis=2, tiled=True),
        lax.all_gather(out_weight, "dp", axis=1, tiled=True),
        lax.all_gather(fc1_weight, "dp", axis=0, tiled=True),
        lax.all_gather(fc1_bias, "dp", axis=1, tiled=True),
        lax.all_gather(fc2_weight, "dp", axis=1, tiled=True),
    )
    model_width = frames.shape[1]
    doc_ids = segments[0]
    seq_length = doc_ids.shape[0]
    heads_width = in_full.shape[2]
    local_heads = heads_width // HD
    block_rows = min(512, seq_length)
    num_blocks = seq_length // block_rows
    rows_in = frames.astype(jnp.float32)
    normed = layer_norm(rows_in, gain_one, shift_one).astype(jnp.bfloat16)
    normed_all = lax.all_gather(normed, "tensor", axis=0, tiled=True)
    projected = jnp.dot(
        normed_all,
        in_full.reshape(model_width, 3 * heads_width),
        preferred_element_type=jnp.float32,
    ).reshape(seq_length, 3, heads_width)
    bias_pair = proj_full.astype(jnp.float32).reshape(2, heads_width)
    query = (
        (projected[:, 0] + bias_pair[0]).astype(jnp.bfloat16).reshape(seq_length, local_heads, HD)
    )
    keys_all = projected[:, 1].astype(jnp.bfloat16).reshape(seq_length, local_heads, HD)
    values_all = (
        (projected[:, 2] + bias_pair[1]).astype(jnp.bfloat16).reshape(seq_length, local_heads, HD)
    )

    def scores_of(query_block, doc_block):
        raw_scores = contract("qhe,khe->hqk", query_block, keys_all) * 0.125
        same_doc = doc_block[:, None] == doc_ids[None, :]
        return jnp.where(same_doc[None], raw_scores, -1e30)

    def forward_block(block_index):
        block_start = block_index * block_rows
        query_block = lax.dynamic_slice_in_dim(query, block_start, block_rows, 0)
        doc_block = lax.dynamic_slice_in_dim(doc_ids, block_start, block_rows, 0)
        scores = scores_of(query_block, doc_block)
        row_max = jnp.max(scores, axis=-1, keepdims=True)
        exp_scores = jnp.exp(scores - row_max)
        row_total = jnp.sum(exp_scores, axis=-1, keepdims=True)
        attn_probs = (exp_scores / row_total).astype(jnp.bfloat16)
        block_mixed = contract("hqk,khe->qhe", attn_probs, values_all)
        log_total = (row_max + jnp.log(row_total))[..., 0]
        return (block_mixed.astype(jnp.bfloat16).reshape(block_rows, heads_width), log_total)

    mixed_blocks, log_totals = lax.map(forward_block, jnp.arange(num_blocks, dtype=jnp.int32))
    attn_mixed = mixed_blocks.reshape(seq_length, heads_width)
    attn_partial = jnp.dot(attn_mixed, out_full, preferred_element_type=jnp.float32)
    attended = lax.psum_scatter(attn_partial, "tensor", scatter_dimension=0, tiled=True) + bias_out
    middle = rows_in + attended
    normed_two = layer_norm(middle, gain_two, shift_two).astype(jnp.bfloat16)
    grad_out = cotangent.astype(jnp.float32)
    normed_two_all = lax.all_gather(normed_two, "tensor", axis=0, tiled=True)
    hidden = jnp.dot(
        normed_two_all, fc1_full, preferred_element_type=jnp.float32
    ) + fc1b_full.astype(jnp.float32).reshape(-1)
    active = gelu_exact(hidden).astype(jnp.bfloat16)
    branch = (
        lax.psum_scatter(
            jnp.dot(active, fc2_full, preferred_element_type=jnp.float32).astype(jnp.bfloat16),
            "tensor",
            scatter_dimension=0,
            tiled=True,
        ).astype(jnp.float32)
        + bias_fc2
    )
    output = (middle + branch).astype(jnp.bfloat16)
    grad_branch_all = lax.all_gather(cotangent, "tensor", axis=0, tiled=True)
    grad_fc2 = contract("lf,ld->fd", active, grad_branch_all)
    grad_active = contract("ld,fd->lf", grad_branch_all, fc2_full)
    grad_hidden = jax.vjp(gelu_exact, hidden)[1](grad_active)[0].astype(jnp.bfloat16)
    grad_fc1 = contract("ld,lf->df", normed_two_all, grad_hidden)
    grad_fc1b = jnp.sum(grad_hidden.astype(jnp.float32), axis=0).reshape(fc1b_full.shape)
    grad_normed_two = lax.psum_scatter(
        contract("lf,df->ld", grad_hidden, fc1_full).astype(jnp.bfloat16),
        "tensor",
        scatter_dimension=0,
        tiled=True,
    ).astype(jnp.float32)
    grad_bias_fc2 = jnp.sum(grad_out, axis=0)
    norm_back_two = jax.vjp(layer_norm, middle, gain_two, shift_two)[1]
    grad_mid_norm, grad_gain_two, grad_shift_two = norm_back_two(grad_normed_two)
    grad_middle = grad_out + grad_mid_norm
    grad_attended = grad_middle.astype(jnp.bfloat16)
    grad_bias_out = jnp.sum(grad_attended.astype(jnp.float32), axis=0)
    grad_att_all = lax.all_gather(grad_attended, "tensor", axis=0, tiled=True)
    grad_out_w = contract("lh,ld->hd", attn_mixed, grad_att_all)
    grad_mixed = (
        contract("ld,hd->lh", grad_att_all, out_full)
        .astype(jnp.bfloat16)
        .reshape(seq_length, local_heads, HD)
    )

    def backward_block(carried, block_index):
        grad_keys_acc, grad_values_acc = carried
        block_start = block_index * block_rows
        query_block = lax.dynamic_slice_in_dim(query, block_start, block_rows, 0)
        doc_block = lax.dynamic_slice_in_dim(doc_ids, block_start, block_rows, 0)
        grad_block = lax.dynamic_slice_in_dim(grad_mixed, block_start, block_rows, 0)
        scores = scores_of(query_block, doc_block)
        attn_probs = jnp.exp(scores - log_totals[block_index][..., None])
        grad_probs = contract("qhe,khe->hqk", grad_block, values_all)
        row_inner = jnp.sum(attn_probs * grad_probs, axis=-1, keepdims=True)
        grad_scores = (attn_probs * (grad_probs - row_inner)).astype(jnp.bfloat16)
        grad_query_block = contract("hqk,khe->qhe", grad_scores, keys_all) * 0.125
        grad_keys_acc = grad_keys_acc + contract("hqk,qhe->khe", grad_scores, query_block) * 0.125
        grad_values_acc = grad_values_acc + contract(
            "hqk,qhe->khe", attn_probs.astype(jnp.bfloat16), grad_block
        )
        return ((grad_keys_acc, grad_values_acc), grad_query_block)

    empty_acc = jnp.zeros((seq_length, local_heads, HD), jnp.float32)
    (grad_keys_all, grad_values_all), grad_query_blocks = lax.scan(
        backward_block, (empty_acc, empty_acc), jnp.arange(num_blocks, dtype=jnp.int32)
    )
    grad_proj = jnp.stack(
        [
            grad_query_blocks.reshape(seq_length, heads_width),
            grad_keys_all.reshape(seq_length, heads_width),
            grad_values_all.reshape(seq_length, heads_width),
        ],
        axis=1,
    ).astype(jnp.bfloat16)
    grad_proj_sums = jnp.sum(grad_proj.astype(jnp.float32), axis=0)
    grad_proj_b = jnp.stack([grad_proj_sums[0], grad_proj_sums[2]], axis=0).reshape(
        2, local_heads, HD
    )
    grad_in_w = contract("ld,lcf->dcf", normed_all, grad_proj)
    grad_normed = lax.psum_scatter(
        contract("lcf,dcf->ld", grad_proj, in_full).astype(jnp.bfloat16),
        "tensor",
        scatter_dimension=0,
        tiled=True,
    ).astype(jnp.float32)
    norm_back_one = jax.vjp(layer_norm, rows_in, gain_one, shift_one)[1]
    grad_rows_norm, grad_gain_one, grad_shift_one = norm_back_one(grad_normed)
    grad_frames = grad_middle + grad_rows_norm
    g_in, g_proj, g_out, g_fc1, g_fc1b, g_fc2 = (
        lax.psum_scatter(grad_in_w, "dp", scatter_dimension=0, tiled=True),
        lax.psum_scatter(grad_proj_b, "dp", scatter_dimension=2, tiled=True),
        lax.psum_scatter(grad_out_w, "dp", scatter_dimension=1, tiled=True),
        lax.psum_scatter(grad_fc1, "dp", scatter_dimension=0, tiled=True),
        lax.psum_scatter(grad_fc1b, "dp", scatter_dimension=1, tiled=True),
        lax.psum_scatter(grad_fc2, "dp", scatter_dimension=1, tiled=True),
    )
    v_gain_one, v_shift_one, v_gain_two, v_shift_two, v_bias_out, v_bias_fc2 = (
        lax.psum_scatter(grad_gain_one, ("dp", "tensor"), scatter_dimension=0, tiled=True),
        lax.psum_scatter(grad_shift_one, ("dp", "tensor"), scatter_dimension=0, tiled=True),
        lax.psum_scatter(grad_gain_two, ("dp", "tensor"), scatter_dimension=0, tiled=True),
        lax.psum_scatter(grad_shift_two, ("dp", "tensor"), scatter_dimension=0, tiled=True),
        lax.psum_scatter(grad_bias_out, ("dp", "tensor"), scatter_dimension=0, tiled=True),
        lax.psum_scatter(grad_bias_fc2, ("dp", "tensor"), scatter_dimension=0, tiled=True),
    )
    return (
        output,
        grad_frames,
        v_gain_one,
        v_shift_one,
        g_in,
        g_proj,
        g_out,
        v_bias_out,
        v_gain_two,
        v_shift_two,
        g_fc1,
        g_fc1b,
        g_fc2,
        v_bias_fc2,
    )


def solution(mesh):
    in_specs = (
        P(("dp", "tensor"), None),
        P("dp", None),
        P(("dp", "tensor")),
        P(("dp", "tensor")),
        P("dp", None, "tensor"),
        P(None, "tensor", "dp"),
        P("tensor", "dp"),
        P(("dp", "tensor")),
        P(("dp", "tensor")),
        P(("dp", "tensor")),
        P("dp", "tensor"),
        P("tensor", "dp"),
        P("tensor", "dp"),
        P(("dp", "tensor")),
        P(("dp", "tensor"), None),
    )
    out_specs = (
        P(("dp", "tensor"), None),
        P(("dp", "tensor"), None),
        P(("dp", "tensor")),
        P(("dp", "tensor")),
        P("dp", None, "tensor"),
        P(None, "tensor", "dp"),
        P("tensor", "dp"),
        P(("dp", "tensor")),
        P(("dp", "tensor")),
        P(("dp", "tensor")),
        P("dp", "tensor"),
        P("tensor", "dp"),
        P("tensor", "dp"),
        P(("dp", "tensor")),
    )
    return jax.shard_map(
        on_device, mesh=mesh, in_specs=in_specs, out_specs=out_specs, check_vma=False
    )
```

profile of v0, /device:TPU:0, one launch (start us, length us, event | category | flops | bytes accessed | tf_op | source)
XLA Modules:
  0.0 845.4 jit_solution(4965968082217313966)
XLA Ops:
  15.0 42.3 %all-reduce.15 = (f32[768]{0:T(1024)S(1)}, f32[768]{0:T(1024)S(1)}, f32[768]{0:T(1024)S(1)}, f32[768]{0:T(1024)S(1)}, f32[768]{0:T(1024)S(1)}) all-reduce(f32[768]{0:T(1024)S(1)} %dynamic-update-slice.1, f32[768]{0:T(1024)S(1)} %dynamic-update-slice, f32[768]{0:T(1024)S(1)} %dynamic-update-slice.2, ...), channel_id=1, replica_groups=mesh['dp'=8,'tensor'=4] {'dp','tensor'}, use_global_device_ids=true, to_apply=%add.1 | all-reduce | flops 3840 | bytes 30720
  59.8 30.4 %all_gather.52 = bf16[2,3,64]{1,0,2:T(2,128)(2,1)S(1)} all-gather(bf16[2,3,8]{1,0,2:T(2,128)(2,1)S(1)} %copy.61), channel_id=1, replica_groups=mesh['dp'=8,'tensor'=4] {'dp'}, dimensions={2}, use_global_device_ids=true | all-gather | bytes 864 | tf_op jit(solution)/shard_map/all_gather | solution.py:51
  90.5 33.8 %all_gather.51 = bf16[768,3,192]{2,0,1:T(8,128)(2,1)S(1)} all-gather(bf16[96,3,192]{2,0,1:T(8,128)(2,1)S(1)} %copy-done.26), channel_id=1, replica_groups=mesh['dp'=8,'tensor'=4] {'dp'}, dimensions={0}, use_global_device_ids=true | all-gather | bytes 995328 | tf_op jit(solution)/shard_map/all_gather | solution.py:50
  125.0 31.0 %all_gather.53 = bf16[192,768]{0,1:T(8,128)(2,1)S(1)} all-gather(bf16[192,96]{0,1:T(8,128)(2,1)S(1)} %copy.65), channel_id=1, replica_groups=mesh['dp'=8,'tensor'=4] {'dp'}, dimensions={1}, use_global_device_ids=true | all-gather | bytes 331776 | tf_op jit(solution)/shard_map/all_gather | solution.py:52
  159.8 34.5 %while.27 = (s32[]{:T(128)}, bf16[3,512,192]{1,2,0:T(8,128)(2,1)}, f32[3,3,512]{2,1,0:T(4,128)}, s32[3]{0:T(128)S(1)}, s32[1536]{0:T(1024)S(1)}, /*index=5*/s32[...) while((s32[]{:T(128)}, bf16[3,512,192]{1,2,0:T(8,128)(2,1)}, ...), condition=%wide.region_5.6_spmd, body=%wide.region_2.5_spmd.sunk | while | flops 633174528 | bytes 33499348 | solution.py:99
  199.3 46.7 %reduce-scatter.13.cloned.1.call-done = f32[384,768]{1,0:T(8,128)} async-done(((f32[1536,768]{1,0:T(8,128)}), f32[384,768]{1,0:T(8,128)}) %reduce-scatter.13.cloned.1.call-update) | async-done | bytes 1179664 | tf_op jit(solution)/shard_map/reduce_scatter | solution.py:102
  250.3 26.5 %all_gather.59 = bf16[12,64]{0,1:T(8,128)(2,1)S(1)} all-gather(bf16[12,8]{0,1:T(8,128)(2,1)S(1)} %copy-done.41), channel_id=1, replica_groups=mesh['dp'=8,'tensor'=4] {'dp'}, dimensions={1}, use_global_device_ids=true | all-gather | bytes 1728 | tf_op jit(solution)/shard_map/all_gather | solution.py:54
  283.1 33.6 %all-gather.13.cloned.1.call-done = bf16[768,768]{0,1:T(8,128)(2,1)} async-done(((bf16[768,96]{0,1:T(8,128)(2,1)}), bf16[768,768]{0,1:T(8,128)(2,1)}) %all-gather.13.cloned.1.call-update) | async-done | bytes 1179664 | tf_op jit(solution)/shard_map/all_gather | solution.py:55
  316.8 24.1 %all-gather.15.cloned.1.call-done = bf16[1536,768]{1,0:T(8,128)(2,1)} async-done(((bf16[384,768]{1,0:T(8,128)(2,1)}), bf16[1536,768]{1,0:T(8,128)(2,1)}) %all-gather.15.cloned.1.call-update) | async-done | bytes 2359312 | tf_op jit(solution)/shard_map/all_gather | solution.py:121
  340.9 16.0 %convert_reduce_fusion = (f32[768]{0:T(1024)}, bf16[1536,768]{1,0:T(8,128)(2,1)S(1)}, f32[1536,768]{1,0:T(8,128)}) fusion(f32[1536,768]{1,0:T(8,128)} %fusion.68, f32[768]{0:T(1024)S(1)} %reshape.224, bf16[1536,768]{1,0:T(8,128)(2,1)} %all-gather.15.cloned.1.call-done, bf16[768,768]{0,1:T(8,128)(2,1)} %all-gather.13.cloned.1.call-done), kind=kOutput, calls=%fused_computation.42 | convolution fusion | flops 1900412160 | bytes 15341568 | tf_op jit(solution)/shard_map/ld,fd->lf/dot_general | solution.py:21
  361.9 33.0 %reduce-scatter.17.cloned.1.call-done = bf16[384,768]{1,0:T(8,128)(2,1)} async-done(((bf16[1536,768]{1,0:T(8,128)(2,1)}), bf16[384,768]{1,0:T(8,128)(2,1)}) %reduce-scatter.17.cloned.1.call-update) | async-done | bytes 589840 | tf_op jit(solution)/shard_map/reduce_scatter | solution.py:127
  401.6 24.1 %all-gather.17.cloned.1.call-done = bf16[1536,768]{1,0:T(8,128)(2,1)} async-done(((bf16[384,768]{1,0:T(8,128)(2,1)}), bf16[1536,768]{1,0:T(8,128)(2,1)}) %all-gather.17.cloned.1.call-update) | async-done | bytes 2359312 | tf_op jit(solution)/shard_map/all_gather | solution.py:139
  433.2 106.5 %while.28 = (s32[]{:T(128)}, f32[1536,3,64]{0,2,1:T(8,128)}, f32[1536,3,64]{0,2,1:T(8,128)S(1)}, bf16[3,512,3,64]{1,3,2,0:T(8,128)(2,1)}, s32[3]{0:T(128)S(1)}, ...) while((s32[]{:T(128)}, f32[1536,3,64]{0,2,1:T(8,128)}, ...), condition=%wide.region_15.16_spmd.clone, body=%wide.region_13.15_spmd.clone.sunk | while | flops 1533540864 | bytes 150903440 | solution.py:166
  442.0 7.2 multiply_reduce_fusion.3
  449.2 9.5 %multiply_convert_fusion.3 = bf16[3,512,1536]{2,1,0:T(8,128)(2,1)} fusion(f32[3,512,1536]{2,1,0:T(8,128)} %get-tuple-element.446, f32[3,512,1536]{2,1,0:T(8,128)} %copy-done, f32[3,512]{1,0:T(4,128)S(1)} %get-tuple-element.447), kind=kLoop, calls=%fused_computation.15.clone.1 | loop fusion | flops 7077888 | bytes 23599104 | tf_op jit(solution)/shard_map/while/body/eval_jaxpr/convert_element_type | solution.py:157
  477.6 7.2 multiply_reduce_fusion.3
  484.8 9.4 %multiply_convert_fusion.3 = bf16[3,512,1536]{2,1,0:T(8,128)(2,1)} fusion(f32[3,512,1536]{2,1,0:T(8,128)} %get-tuple-element.446, f32[3,512,1536]{2,1,0:T(8,128)} %copy-done, f32[3,512]{1,0:T(4,128)S(1)} %get-tuple-element.447), kind=kLoop, calls=%fused_computation.15.clone.1 | loop fusion | flops 7077888 | bytes 23599104 | tf_op jit(solution)/shard_map/while/body/eval_jaxpr/convert_element_type | solution.py:157
  513.1 7.2 multiply_reduce_fusion.3
  520.3 9.4 %multiply_convert_fusion.3 = bf16[3,512,1536]{2,1,0:T(8,128)(2,1)} fusion(f32[3,512,1536]{2,1,0:T(8,128)} %get-tuple-element.446, f32[3,512,1536]{2,1,0:T(8,128)} %copy-done, f32[3,512]{1,0:T(4,128)S(1)} %get-tuple-element.447), kind=kLoop, calls=%fused_computation.15.clone.1 | loop fusion | flops 7077888 | bytes 23599104 | tf_op jit(solution)/shard_map/while/body/eval_jaxpr/convert_element_type | solution.py:157
  586.8 37.1 %all-reduce.16 = (f32[2,3,64]{2,1,0:T(4,128)S(1)}, f32[12,64]{1,0:T(8,128)S(1)}) all-reduce(f32[2,3,64]{2,1,0:T(4,128)S(1)} %reshape.222, f32[12,64]{1,0:T(8,128)} %reshape.223), channel_id=9, replica_groups=mesh['dp'=8,'tensor'=4] {'dp'}, use_global_device_ids=true, to_apply=%region_25.26.clone | all-reduce | flops 1152 | bytes 9216
  635.4 38.0 %all-reduce.14 = (f32[768]{0:T(1024)S(1)}, f32[768]{0:T(1024)S(1)}, f32[768]{0:T(1024)S(1)}, f32[768]{0:T(1024)S(1)}, f32[768]{0:T(1024)S(1)}, /*index=5*/f32[768]{0:T(1024)S(1)}, f32[768]{0:T(1024)S(1)}) all-reduce(f32[768]{0:T(1024)} %dynamic-update-slice.5, ...), channel_id=1, replica_groups=mesh['dp'=8,'tensor'=4] {'dp','tensor'}, use_global_device_ids=true, to_apply=%add.5 | all-reduce | flops 5376 | bytes 43008
  678.9 14.2 %reduce-scatter.25.cloned.1.call-done = f32[768,96]{0,1:T(8,128)} async-done(((f32[768,768]{0,1:T(8,128)}), f32[768,96]{0,1:T(8,128)}) %reduce-scatter.25.cloned.1.call-update) | async-done | bytes 294928 | tf_op jit(solution)/shard_map/reduce_scatter | solution.py:197
  693.1 72.5 %reduce-scatter.23.cloned.1.call-done = f32[96,768]{1,0:T(8,128)} async-done(((f32[768,768]{1,0:T(8,128)}), f32[96,768]{1,0:T(8,128)}) %reduce-scatter.23.cloned.1.call-update) | async-done | bytes 294928 | tf_op jit(solution)/shard_map/reduce_scatter | solution.py:195
  765.5 72.3 %reduce-scatter.21.cloned.1.call-done = f32[96,3,192]{2,0,1:T(8,128)} async-done(((f32[768,3,192]{2,0,1:T(8,128)}), f32[96,3,192]{2,0,1:T(8,128)}) %reduce-scatter.21.cloned.1.call-update) | async-done | bytes 221200 | tf_op jit(solution)/shard_map/reduce_scatter | solution.py:192
  (308 shorter events, 192.8 us)
Async XLA Ops:
  8.0 51.6 %copy-start.42 = (bf16[2,3,8]{2,0,1:T(2,128)(2,1)S(1)}, bf16[2,3,8]{2,0,1:T(2,128)(2,1)}, u32[]{:S(2)}) copy-start(bf16[2,3,8]{2,0,1:T(2,128)(2,1)} %param.24) | copy-start | bytes 292
  8.0 51.7 %copy-start.23 = (s32[1,1536]{1,0:T(1,128)S(1)}, s32[1,1536]{1,0:T(1,128)}, u32[]{:S(2)}) copy-start(s32[1,1536]{1,0:T(1,128)} %param.20) | copy-start | bytes 18436
  8.0 82.3 %copy-start.33 = (bf16[192,96]{1,0:T(8,128)(2,1)S(1)}, bf16[192,96]{1,0:T(8,128)(2,1)}, u32[]{:S(2)}) copy-start(bf16[192,96]{1,0:T(8,128)(2,1)} %param.25) | copy-start | bytes 110596
  8.0 82.4 %copy-start.26 = (bf16[96,3,192]{2,0,1:T(8,128)(2,1)S(1)}, bf16[96,3,192]{2,0,1:T(8,128)(2,1)}, u32[]{:S(2)}) copy-start(bf16[96,3,192]{2,0,1:T(8,128)(2,1)} %param.23) | copy-start | bytes 331780
  8.1 147.9 %all-gather.7.cloned.1.call-start = ((), (), s32[]{:S(2)}) async-start(), calls=%async_computation.8 | async-start | bytes 2949120 | tf_op jit(solution)/shard_map/all_gather | solution.py:66
  9.4 50.4 %copy-start.29 = (f32[384]{0:T(512)}, f32[384]{0:T(512)S(1)}, u32[]{:S(2)}) copy-start(f32[384]{0:T(512)S(1)} %broadcast_multiply_fusion.1) | copy-start | bytes 4612
  10.8 49.0 %copy-start.34 = (f32[384]{0:T(512)}, f32[384]{0:T(512)S(1)}, u32[]{:S(2)}) copy-start(f32[384]{0:T(512)S(1)} %fusion.58) | copy-start | bytes 4612
  59.5 186.5 %reduce-scatter.13.cloned.1.call-start = ((), (), s32[]{:S(2)}) async-start(), calls=%async_computation.9 | async-start | bytes 5898240 | tf_op jit(solution)/shard_map/reduce_scatter | solution.py:102
  198.6 78.3 %all-gather.11.cloned.1.call-start = ((), (), s32[]{:S(2)}) async-start(), calls=%async_computation.11 | async-start | bytes 1327104 | tf_op jit(solution)/shard_map/all_gather | solution.py:53
  199.2 77.8 %all-gather.9.cloned.1.call-start = ((), (), s32[]{:S(2)}) async-start(), calls=%async_computation.10 | async-start | bytes 2949120 | tf_op jit(solution)/shard_map/all_gather | solution.py:106
  248.9 67.9 %all-gather.13.cloned.1.call-start = ((), (), s32[]{:S(2)}) async-start(), calls=%async_computation.12 | async-start | bytes 1327104 | tf_op jit(solution)/shard_map/all_gather | solution.py:55
  249.5 91.4 %all-gather.15.cloned.1.call-start = ((), (), s32[]{:S(2)}) async-start(), calls=%async_computation.14 | async-start | bytes 2949120 | tf_op jit(solution)/shard_map/all_gather | solution.py:121
  250.2 144.8 %reduce-scatter.17.cloned.1.call-start = ((), (), s32[]{:S(2)}) async-start(), calls=%async_computation.15 | async-start | bytes 2949120 | tf_op jit(solution)/shard_map/reduce_scatter | solution.py:127
  276.9 63.9 %copy-start.39 = (f32[768]{0:T(1024)}, f32[768]{0:T(1024)S(1)}, u32[]{:S(2)}) copy-start(f32[768]{0:T(1024)S(1)} %reshape.224) | copy-start | bytes 9220
  361.9 63.8 %all-gather.17.cloned.1.call-start = ((), (), s32[]{:S(2)}) async-start(), calls=%async_computation.16 | async-start | bytes 2949120 | tf_op jit(solution)/shard_map/all_gather | solution.py:139
  401.5 223.8 %reduce-scatter.27.cloned.1.call-start = ((), (), s32[]{:S(2)}) async-start(), calls=%async_computation.21 | async-start | bytes 884736
  429.5 197.4 %reduce-scatter.19.cloned.1.call-start = ((), (), s32[]{:S(2)}) async-start(), calls=%async_computation.17 | async-start | bytes 2949120 | tf_op jit(solution)/shard_map/reduce_scatter | solution.py:182
  550.8 126.1 %reduce-scatter.15.cloned.1.call-start = ((), (), s32[]{:S(2)}) async-start(), calls=%async_computation.13 | async-start | bytes 2949120 | tf_op jit(solution)/shard_map/reduce_scatter | solution.py:112
  560.9 132.2 %reduce-scatter.25.cloned.1.call-start = ((), (), s32[]{:S(2)}) async-start(), calls=%async_computation.20 | async-start | bytes 2654208 | tf_op jit(solution)/shard_map/reduce_scatter | solution.py:197
  566.8 198.7 %reduce-scatter.23.cloned.1.call-start = ((), (), s32[]{:S(2)}) async-start(), calls=%async_computation.19 | async-start | bytes 2654208 | tf_op jit(solution)/shard_map/reduce_scatter | solution.py:195
  573.1 264.7 %reduce-scatter.21.cloned.1.call-start = ((), (), s32[]{:S(2)}) async-start(), calls=%async_computation.18 | async-start | bytes 2654208 | tf_op jit(solution)/shard_map/reduce_scatter | solution.py:192
  579.7 50.0 %copy-start.35 = (f32[384]{0:T(512)S(1)}, f32[384]{0:T(512)}, u32[]{:S(2)}) copy-start(f32[384]{0:T(512)} %copy-done.34) | copy-start | bytes 4612
  579.8 52.4 %copy-start.8 = (f32[384,768]{1,0:T(8,128)S(1)}, f32[384,768]{1,0:T(8,128)}, u32[]{:S(2)}) copy-start(f32[384,768]{1,0:T(8,128)} %copy-done.7) | copy-start | bytes 3538948
  579.8 52.4 %copy-start.37 = (f32[384]{0:T(512)S(1)}, f32[384]{0:T(512)}, u32[]{:S(2)}) copy-start(f32[384]{0:T(512)} %copy-done.36) | copy-start | bytes 4612
  (57 other events, 473.4 us)
Sparse Core Ops, SparseCore 0:
  59.6 23.9 all-gather.6
  198.7 47.1 reduce-scatter.12
  401.6 24.0 all-gather.16
Sparse Core Ops, SparseCore 1:
  201.5 40.8 all-gather.10
  249.0 23.9 all-gather.8
  275.2 41.5 all-gather.12
  318.4 22.4 all-gather.14
  362.0 32.9 reduce-scatter.16
  429.6 62.5 reduce-scatter.26
  550.9 33.0 reduce-scatter.18
  586.3 33.0 reduce-scatter.14
  623.7 69.3 reduce-scatter.24
  697.6 67.9 reduce-scatter.22
  769.9 67.9 reduce-scatter.20
where the time goes:
time: 856 us; the launch traced here: 845 us
  waiting for transfers between devices  322 us (38%)
  blocking collectives  239 us (28%)
  matrix products  135 us (16%)
  other arithmetic  77.1 us (9%)
  local copies, waits for them, and re-layouts  43.6 us (5%)
  between operations  16.9 us (2%)
  loops' own time  10.2 us (1%)
    unnamed x3, blocking collectives  117 us
    dot_general x28, matrix products, contract(): return jnp.einsum(pattern, left, right, preferred_element_type=jnp.float32)  115 us
    reduce_scatter x1, waiting for transfers between devices, on_device(): lax.psum_scatter(grad_fc1, 'dp', scatter_dimension=0, tiled=True)  72.5 us
    reduce_scatter x1, waiting for transfers between devices, on_device(): lax.psum_scatter(grad_in_w, 'dp', scatter_dimension=0, tiled=True)  72.3 us
    reduce_scatter x1, waiting for transfers between devices, on_device(): lax.psum_scatter(attn_partial, 'tensor', scatter_dimension=0, tiled=True)  46.7 us
    all_gather x1, blocking collectives, on_device(): lax.all_gather(in_weight, 'dp', axis=0, tiled=True)  33.8 us
    all_gather x1, waiting for transfers between devices, on_device(): lax.all_gather(fc2_weight, 'dp', axis=1, tiled=True)  33.6 us
    reduce_scatter x1, waiting for transfers between devices, on_device(): lax.psum_scatter(contract('lf,df->ld', grad_hidden, fc1_full).astype(jnp....  33 us
  transfers between devices with their start and end apart: 14, of which 8 were waited for; matrix products, arithmetic and copies ran while one was open for 20% of the time, Pallas kernels for 0%

commit v1 on v0

--- a/solution.py
+++ b/solution.py
@@ -4,6 +4,28 @@
 from jax.sharding import PartitionSpec as P
 
 HD = 64
+
+
+def laid_out(blocks, dim):
+    blocks = jnp.moveaxis(blocks, 0, dim)
+    shape = blocks.shape
+    return blocks.reshape(*shape[:dim], shape[dim] * shape[dim + 1], *shape[dim + 2 :])
+
+
+def gather_around(x, axis, dim):
+    devices = lax.axis_size(axis)
+    pairs = [(i, (i + 1) % devices) for i in range(devices)]
+    back = [(b, a) for a, b in pairs]
+    lower, upper = ([], [])
+    for turn in range(devices - 1):
+        if turn % 2 == 0:
+            lower.append(lax.ppermute(lower[-1] if lower else x, axis, pairs))
+        else:
+            upper.append(lax.ppermute(upper[-1] if upper else x, axis, back))
+    pieces = jnp.stack([*lower[::-1], x, *upper])
+    shift = lax.axis_index(axis) - len(lower)
+    pieces = pieces[(jnp.arange(devices) - shift) % devices]
+    return laid_out(pieces, dim)
 
 
 def layer_norm(row_block, norm_gain, norm_shift):
@@ -47,7 +69,7 @@
         lax.all_gather(fc2_bias, ("dp", "tensor"), axis=0, tiled=True),
     )
     in_full, proj_full, out_full, fc1_full, fc1b_full, fc2_full = (
-        lax.all_gather(in_weight, "dp", axis=0, tiled=True),
+        gather_around(in_weight, "dp", 0),
         lax.all_gather(proj_bias, "dp", axis=2, tiled=True),
         lax.all_gather(out_weight, "dp", axis=1, tiled=True),
         lax.all_gather(fc1_weight, "dp", axis=0, tiled=True),

time: 856 us -> 843 us (0.985)
  blocking collectives: 239 us -> 206 us
  starting transfers between devices: 0.98 us -> 15.9 us
    all_gather x1 -> x0, blocking collectives: 33.8 us -> none  [on_device(): lax.all_gather(in_weight, 'dp', axis=0, tiled=True)]
    ppermute x0 -> x7, starting transfers between devices: none -> 14.9 us  [the longest x3 11.6 us: gather_around(): upper.append(lax.ppermute(upper[-1] if upper else x, axis, back))]
    unnamed x100 -> x109, local copies, waits for them, and re-layouts: 20.8 us -> 23.9 us
  transfers between devices with their start and end apart: 14 -> 21, of which waited for: 8 -> 10; matrix products, arithmetic and copies ran while one was open for 20% -> 21% of each run, Pallas kernels for 0% -> 0%
where the time goes in v1:
time: 843 us; the launch traced here: 837 us
  waiting for transfers between devices  326 us (39%)
  blocking collectives  206 us (24%)
  matrix products  133 us (16%)
  other arithmetic  76.9 us (9%)
  local copies, waits for them, and re-layouts  51.2 us (6%)
  between operations  17.3 us (2%)
  starting transfers between devices  15.9 us (2%)
  loops' own time  10.2 us (1%)
    unnamed x3, blocking collectives  117 us
    dot_general x28, matrix products, contract(): return jnp.einsum(pattern, left, right, preferred_element_type=jnp.float32)  114 us
    reduce_scatter x1, waiting for transfers between devices, on_device(): lax.psum_scatter(grad_fc1, 'dp', scatter_dimension=0, tiled=True)  72.4 us
    reduce_scatter x1, waiting for transfers between devices, on_device(): lax.psum_scatter(grad_in_w, 'dp', scatter_dimension=0, tiled=True)  72.4 us
    reduce_scatter x1, waiting for transfers between devices, on_device(): lax.psum_scatter(attn_partial, 'tensor', scatter_dimension=0, tiled=True)  50 us
    all_gather x1, waiting for transfers between devices, on_device(): lax.all_gather(fc2_weight, 'dp', axis=1, tiled=True)  33.9 us
    reduce_scatter x1, waiting for transfers between devices, on_device(): lax.psum_scatter(contract('lf,df->ld', grad_hidden, fc1_full).astype(jnp....  33.1 us
    all_gather x1, blocking collectives, on_device(): lax.all_gather(out_weight, 'dp', axis=1, tiled=True)  32.3 us
  transfers between devices with their start and end apart: 21, of which 10 were waited for; matrix products, arithmetic and copies ran while one was open for 21% of the time, Pallas kernels for 0%

profile of v1, /device:TPU:0, one launch (start us, length us, event | category | flops | bytes accessed | tf_op | source)
XLA Modules:
  0.0 837.4 jit_solution(4911257499384798782)
XLA Ops:
  15.0 42.3 %all-reduce.15 = (f32[768]{0:T(1024)S(1)}, f32[768]{0:T(1024)S(1)}, f32[768]{0:T(1024)S(1)}, f32[768]{0:T(1024)S(1)}, f32[768]{0:T(1024)S(1)}) all-reduce(f32[768]{0:T(1024)S(1)} %dynamic-update-slice.1, f32[768]{0:T(1024)S(1)} %dynamic-update-slice, f32[768]{0:T(1024)S(1)} %dynamic-update-slice.2, ...), channel_id=1, replica_groups=mesh['dp'=8,'tensor'=4] {'dp','tensor'}, use_global_device_ids=true, to_apply=%add.1 | all-reduce | flops 3840 | bytes 30720
  64.5 30.4 %all_gather.48 = bf16[2,3,64]{1,0,2:T(2,128)(2,1)S(1)} all-gather(bf16[2,3,8]{1,0,2:T(2,128)(2,1)S(1)} %copy.64), channel_id=1, replica_groups=mesh['dp'=8,'tensor'=4] {'dp'}, dimensions={2}, use_global_device_ids=true | all-gather | bytes 864 | tf_op jit(solution)/shard_map/all_gather | solution.py:73
  95.3 32.3 %all_gather.49 = bf16[192,768]{0,1:T(8,128)(2,1)S(1)} all-gather(bf16[192,96]{0,1:T(8,128)(2,1)S(1)} %copy.68), channel_id=1, replica_groups=mesh['dp'=8,'tensor'=4] {'dp'}, dimensions={1}, use_global_device_ids=true | all-gather | bytes 331776 | tf_op jit(solution)/shard_map/all_gather | solution.py:74
  150.3 34.5 %while.27 = (s32[]{:T(128)}, bf16[3,512,192]{1,2,0:T(8,128)(2,1)}, f32[3,3,512]{2,1,0:T(4,128)}, s32[3]{0:T(128)S(1)}, s32[1536]{0:T(1024)S(1)}, /*index=5*/s32[...) while((s32[]{:T(128)}, bf16[3,512,192]{1,2,0:T(8,128)(2,1)}, ...), condition=%wide.region_5.6_spmd, body=%wide.region_2.5_spmd.sunk | while | flops 633174528 | bytes 33499348 | solution.py:121
  189.7 50.0 %reduce-scatter.13.cloned.1.call-done = f32[384,768]{1,0:T(8,128)} async-done(((f32[1536,768]{1,0:T(8,128)}), f32[384,768]{1,0:T(8,128)}) %reduce-scatter.13.cloned.1.call-update) | async-done | bytes 1179664 | tf_op jit(solution)/shard_map/reduce_scatter | solution.py:124
  244.0 26.2 %all_gather.55 = bf16[12,64]{0,1:T(8,128)(2,1)S(1)} all-gather(bf16[12,8]{0,1:T(8,128)(2,1)S(1)} %copy-done.42), channel_id=1, replica_groups=mesh['dp'=8,'tensor'=4] {'dp'}, dimensions={1}, use_global_device_ids=true | all-gather | bytes 1728 | tf_op jit(solution)/shard_map/all_gather | solution.py:76
  270.4 6.2 fusion.69
  276.6 33.9 %all-gather.13.cloned.1.call-done = bf16[768,768]{0,1:T(8,128)(2,1)} async-done(((bf16[768,96]{0,1:T(8,128)(2,1)}), bf16[768,768]{0,1:T(8,128)(2,1)}) %all-gather.13.cloned.1.call-update) | async-done | bytes 1179664 | tf_op jit(solution)/shard_map/all_gather | solution.py:77
  310.5 24.1 %all-gather.15.cloned.1.call-done = bf16[1536,768]{1,0:T(8,128)(2,1)} async-done(((bf16[384,768]{1,0:T(8,128)(2,1)}), bf16[1536,768]{1,0:T(8,128)(2,1)}) %all-gather.15.cloned.1.call-update) | async-done | bytes 2359312 | tf_op jit(solution)/shard_map/all_gather | solution.py:143
  334.6 16.1 %convert_reduce_fusion = (f32[768]{0:T(1024)}, bf16[1536,768]{1,0:T(8,128)(2,1)S(1)}, f32[1536,768]{1,0:T(8,128)}) fusion(f32[1536,768]{1,0:T(8,128)} %fusion.69, f32[768]{0:T(1024)S(1)} %reshape.273, bf16[1536,768]{1,0:T(8,128)(2,1)} %all-gather.15.cloned.1.call-done, bf16[768,768]{0,1:T(8,128)(2,1)} %all-gather.13.cloned.1.call-done), kind=kOutput, calls=%fused_computation.43 | convolution fusion | flops 1900412160 | bytes 15341568 | tf_op jit(solution)/shard_map/ld,fd->lf/dot_general | solution.py:43
  355.7 33.1 %reduce-scatter.17.cloned.1.call-done = bf16[384,768]{1,0:T(8,128)(2,1)} async-done(((bf16[1536,768]{1,0:T(8,128)(2,1)}), bf16[384,768]{1,0:T(8,128)(2,1)}) %reduce-scatter.17.cloned.1.call-update) | async-done | bytes 589840 | tf_op jit(solution)/shard_map/reduce_scatter | solution.py:149
  398.3 21.2 %all-gather.17.cloned.1.call-done = bf16[1536,768]{1,0:T(8,128)(2,1)} async-done(((bf16[384,768]{1,0:T(8,128)(2,1)}), bf16[1536,768]{1,0:T(8,128)(2,1)}) %all-gather.17.cloned.1.call-update) | async-done | bytes 2359312 | tf_op jit(solution)/shard_map/all_gather | solution.py:161
  427.0 106.5 %while.28 = (s32[]{:T(128)}, f32[1536,3,64]{0,2,1:T(8,128)}, f32[1536,3,64]{0,2,1:T(8,128)S(1)}, bf16[3,512,3,64]{1,3,2,0:T(8,128)(2,1)}, s32[3]{0:T(128)S(1)}, ...) while((s32[]{:T(128)}, f32[1536,3,64]{0,2,1:T(8,128)}, ...), condition=%wide.region_15.16_spmd.clone, body=%wide.region_13.15_spmd.clone.sunk | while | flops 1533540864 | bytes 150903440 | solution.py:188
  435.9 7.2 multiply_reduce_fusion.3
  443.1 9.4 %multiply_convert_fusion.3 = bf16[3,512,1536]{2,1,0:T(8,128)(2,1)} fusion(f32[3,512,1536]{2,1,0:T(8,128)} %get-tuple-element.446, f32[3,512,1536]{2,1,0:T(8,128)} %copy-done, f32[3,512]{1,0:T(4,128)S(1)} %get-tuple-element.447), kind=kLoop, calls=%fused_computation.16.clone.1 | loop fusion | flops 7077888 | bytes 23599104 | tf_op jit(solution)/shard_map/while/body/eval_jaxpr/convert_element_type | solution.py:179
  471.4 7.2 multiply_reduce_fusion.3
  478.6 9.4 %multiply_convert_fusion.3 = bf16[3,512,1536]{2,1,0:T(8,128)(2,1)} fusion(f32[3,512,1536]{2,1,0:T(8,128)} %get-tuple-element.446, f32[3,512,1536]{2,1,0:T(8,128)} %copy-done, f32[3,512]{1,0:T(4,128)S(1)} %get-tuple-element.447), kind=kLoop, calls=%fused_computation.16.clone.1 | loop fusion | flops 7077888 | bytes 23599104 | tf_op jit(solution)/shard_map/while/body/eval_jaxpr/convert_element_type | solution.py:179
  506.9 7.2 multiply_reduce_fusion.3
  514.2 9.4 %multiply_convert_fusion.3 = bf16[3,512,1536]{2,1,0:T(8,128)(2,1)} fusion(f32[3,512,1536]{2,1,0:T(8,128)} %get-tuple-element.446, f32[3,512,1536]{2,1,0:T(8,128)} %copy-done, f32[3,512]{1,0:T(4,128)S(1)} %get-tuple-element.447), kind=kLoop, calls=%fused_computation.16.clone.1 | loop fusion | flops 7077888 | bytes 23599104 | tf_op jit(solution)/shard_map/while/body/eval_jaxpr/convert_element_type | solution.py:179
  579.3 37.0 %all-reduce.16 = (f32[2,3,64]{2,1,0:T(4,128)}, f32[12,64]{1,0:T(8,128)}) all-reduce(f32[2,3,64]{2,1,0:T(4,128)} %reshape.271, f32[12,64]{1,0:T(8,128)} %reshape.272), channel_id=9, replica_groups=mesh['dp'=8,'tensor'=4] {'dp'}, use_global_device_ids=true, to_apply=%region_25.26.clone | all-reduce | flops 1152 | bytes 9216
  629.6 37.8 %all-reduce.14 = (f32[768]{0:T(1024)S(1)}, f32[768]{0:T(1024)S(1)}, f32[768]{0:T(1024)S(1)}, f32[768]{0:T(1024)S(1)}, f32[768]{0:T(1024)S(1)}, /*index=5*/f32[768]{0:T(1024)S(1)}, f32[768]{0:T(1024)S(1)}) all-reduce(f32[768]{0:T(1024)} %dynamic-update-slice.5, ...), channel_id=1, replica_groups=mesh['dp'=8,'tensor'=4] {'dp','tensor'}, use_global_device_ids=true, to_apply=%add.5 | all-reduce | flops 5376 | bytes 43008
  673.0 11.9 %reduce-scatter.25.cloned.1.call-done = f32[768,96]{0,1:T(8,128)} async-done(((f32[768,768]{0,1:T(8,128)}), f32[768,96]{0,1:T(8,128)}) %reduce-scatter.25.cloned.1.call-update) | async-done | bytes 294928 | tf_op jit(solution)/shard_map/reduce_scatter | solution.py:219
  684.9 72.4 %reduce-scatter.23.cloned.1.call-done = f32[96,768]{1,0:T(8,128)} async-done(((f32[768,768]{1,0:T(8,128)}), f32[96,768]{1,0:T(8,128)}) %reduce-scatter.23.cloned.1.call-update) | async-done | bytes 294928 | tf_op jit(solution)/shard_map/reduce_scatter | solution.py:217
  757.3 72.4 %reduce-scatter.21.cloned.1.call-done = f32[96,3,192]{2,0,1:T(8,128)} async-done(((f32[768,3,192]{2,0,1:T(8,128)}), f32[96,3,192]{2,0,1:T(8,128)}) %reduce-scatter.21.cloned.1.call-update) | async-done | bytes 221200 | tf_op jit(solution)/shard_map/reduce_scatter | solution.py:214
  (336 shorter events, 212.8 us)
Async XLA Ops:
  8.0 86.9 %copy-start.24 = (s32[1,1536]{1,0:T(1,128)S(1)}, s32[1,1536]{1,0:T(1,128)}, u32[]{:S(2)}) copy-start(s32[1,1536]{1,0:T(1,128)} %param.20) | copy-start | bytes 18436
  8.0 87.1 %copy-start.34 = (bf16[192,96]{1,0:T(8,128)(2,1)S(1)}, bf16[192,96]{1,0:T(8,128)(2,1)}, u32[]{:S(2)}) copy-start(bf16[192,96]{1,0:T(8,128)(2,1)} %param.25) | copy-start | bytes 110596
  8.1 138.5 %all-gather.7.cloned.1.call-start = ((), (), s32[]{:S(2)}) async-start(), calls=%async_computation.8 | async-start | bytes 2949120 | tf_op jit(solution)/shard_map/all_gather | solution.py:88
  59.5 180.2 %reduce-scatter.13.cloned.1.call-start = ((), (), s32[]{:S(2)}) async-start(), calls=%async_computation.9 | async-start | bytes 5898240 | tf_op jit(solution)/shard_map/reduce_scatter | solution.py:124
  59.6 35.7 %collective-permute-start = (bf16[96,3,192]{2,0,1:T(8,128)(2,1)S(1)}, bf16[96,3,192]{2,0,1:T(8,128)(2,1)S(1)}, u32[]{:S(2)}, u32[]{:S(2)}) collective-permute-start(bf16[96,3,192]{2,0,1:T(8,128)(2,1)S(1)} %copy-done.27), channel_id=1, source_target_pairs={{0,4},{4,8},{8,12},{12,16},{16,20},{20,24},{24,28},{28,0},{1,5},{5... | collective-permute-start | bytes 331784 | tf_op jit(solution)/shard_map/ppermute | solution.py:22
  61.9 66.7 %collective-permute-start.4 = (bf16[96,3,192]{2,0,1:T(8,128)(2,1)S(1)}, bf16[96,3,192]{2,0,1:T(8,128)(2,1)S(1)}, u32[]{:S(2)}, u32[]{:S(2)}) collective-permute-start(bf16[96,3,192]{2,0,1:T(8,128)(2,1)S(1)} %copy-done.27), channel_id=1, source_target_pairs={{4,0},{8,4},{12,8},{16,12},{20,16},{24,20},{28,24},{0,28},{5,1},{9... | collective-permute-start | bytes 331784 | tf_op jit(solution)/shard_map/ppermute | solution.py:24
  95.3 32.4 %collective-permute-start.1 = (bf16[96,3,192]{2,0,1:T(8,128)(2,1)S(1)}, bf16[96,3,192]{2,0,1:T(8,128)(2,1)S(1)}, u32[]{:S(2)}, u32[]{:S(2)}) collective-permute-start(bf16[96,3,192]{2,0,1:T(8,128)(2,1)S(1)} %collective-permute-done), channel_id=1, source_target_pairs={{0,4},{4,8},{8,12},{12,16},{16,20},{20,24},{24,28},{28,0},{1,5},{5... | collective-permute-start | bytes 331784 | tf_op jit(solution)/shard_map/ppermute | solution.py:22
  127.7 7.8 collective-permute-start.2
  128.6 6.9 collective-permute-start.5
  135.5 7.8 collective-permute-start.3
  135.5 8.0 collective-permute-start.6
  189.1 81.3 %all-gather.11.cloned.1.call-start = ((), (), s32[]{:S(2)}) async-start(), calls=%async_computation.11 | async-start | bytes 1327104 | tf_op jit(solution)/shard_map/all_gather | solution.py:75
  189.7 80.7 %all-gather.9.cloned.1.call-start = ((), (), s32[]{:S(2)}) async-start(), calls=%async_computation.10 | async-start | bytes 2949120 | tf_op jit(solution)/shard_map/all_gather | solution.py:128
  242.6 67.9 %all-gather.13.cloned.1.call-start = ((), (), s32[]{:S(2)}) async-start(), calls=%async_computation.12 | async-start | bytes 1327104 | tf_op jit(solution)/shard_map/all_gather | solution.py:77
  243.2 91.4 %all-gather.15.cloned.1.call-start = ((), (), s32[]{:S(2)}) async-start(), calls=%async_computation.14 | async-start | bytes 2949120 | tf_op jit(solution)/shard_map/all_gather | solution.py:143
  243.9 144.9 %reduce-scatter.17.cloned.1.call-start = ((), (), s32[]{:S(2)}) async-start(), calls=%async_computation.15 | async-start | bytes 2949120 | tf_op jit(solution)/shard_map/reduce_scatter | solution.py:149
  270.4 64.2 %copy-start.40 = (f32[768]{0:T(1024)}, f32[768]{0:T(1024)S(1)}, u32[]{:S(2)}) copy-start(f32[768]{0:T(1024)S(1)} %reshape.273) | copy-start | bytes 9220
  355.7 63.8 %all-gather.17.cloned.1.call-start = ((), (), s32[]{:S(2)}) async-start(), calls=%async_computation.16 | async-start | bytes 2949120 | tf_op jit(solution)/shard_map/all_gather | solution.py:161
  395.3 225.1 %reduce-scatter.27.cloned.1.call-start = ((), (), s32[]{:S(2)}) async-start(), calls=%async_computation.21 | async-start | bytes 884736
  423.3 198.8 %reduce-scatter.19.cloned.1.call-start = ((), (), s32[]{:S(2)}) async-start(), calls=%async_computation.17 | async-start | bytes 2949120 | tf_op jit(solution)/shard_map/reduce_scatter | solution.py:204
  542.8 128.2 %reduce-scatter.15.cloned.1.call-start = ((), (), s32[]{:S(2)}) async-start(), calls=%async_computation.13 | async-start | bytes 2949120 | tf_op jit(solution)/shard_map/reduce_scatter | solution.py:134
  551.5 133.4 %reduce-scatter.25.cloned.1.call-start = ((), (), s32[]{:S(2)}) async-start(), calls=%async_computation.20 | async-start | bytes 2654208 | tf_op jit(solution)/shard_map/reduce_scatter | solution.py:219
  556.8 200.5 %reduce-scatter.23.cloned.1.call-start = ((), (), s32[]{:S(2)}) async-start(), calls=%async_computation.19 | async-start | bytes 2654208 | tf_op jit(solution)/shard_map/reduce_scatter | solution.py:217
  563.6 266.0 %reduce-scatter.21.cloned.1.call-start = ((), (), s32[]{:S(2)}) async-start(), calls=%async_computation.18 | async-start | bytes 2654208 | tf_op jit(solution)/shard_map/reduce_scatter | solution.py:214
  (65 other events, 923.1 us)
Sparse Core Ops, SparseCore 0:
  59.6 23.9 all-gather.6
  189.2 50.4 reduce-scatter.12
  395.4 24.0 all-gather.16
Sparse Core Ops, SparseCore 1:
  192.0 44.1 all-gather.10
  242.7 23.9 all-gather.8
  268.9 41.5 all-gather.12
  312.1 22.4 all-gather.14
  355.8 33.0 reduce-scatter.16
  423.4 62.5 reduce-scatter.26
  542.9 32.9 reduce-scatter.18
  578.3 33.0 reduce-scatter.14
  615.6 69.2 reduce-scatter.24
  689.4 67.9 reduce-scatter.22
  761.6 68.0 reduce-scatter.20
